TPU v7x, 256 devices: a whole 4x4x8 slice. The times are simulated.
256 devices in a mesh: row: 32 (over y, z_lo, core), col: 8 (over x, z_hi).
Axes of the slice: x: 4, y: 4, z: 8 (z_hi: 2, z_lo: 4; z = z_hi * 4 + z_lo), core: 2. Of those that a mesh axis runs over, the one named last changes fastest.
Arguments:
- weight: float32 [8192, 4096], P('row', 'col'), may hold values from -0.0625 to 0.0625
- grad: bfloat16 [8192, 4096], P('row', 'col'), may hold values from -6 to 6
- left: bfloat16 [8192, 8192], P('row', 'col'), may hold values from -0.25 to 3, as said below
- right: bfloat16 [4096, 4096], P('row', 'col'), may hold values from -0.25 to 3, as said below
- tokens: bfloat16 [4096, 8192], P('row'), may hold values from -6 to 6
Outputs:
- new_weight: float32 [8192, 4096], P('row', 'col')
- output: bfloat16 [4096, 4096], P('row', 'col')
Inputs may be any that keep to these rules, and one draw needn't show every extreme that they name: left is symmetric. right is symmetric.
All inputs are finite; a program needn't handle non-finite values.
Results may differ from a plain program's by a relative error of at most 0.0056.
Values may be sent and summed in bfloat16 or wider, within the bound.
A program may use at most 64 MiB of HBM per device.

v0:
```python
import jax
import jax.numpy as jnp
from jax import lax
from jax.sharding import PartitionSpec as P


def shards(weight, grad, left, right, tokens):
    left_panel = lax.all_gather(left, "col", axis=1, tiled=True)
    left_total = jnp.dot(
        left_panel,
        lax.all_gather(grad, "row", axis=0, tiled=True),
        preferred_element_type=jnp.float32,
    )
    left_grad = left_total.astype(jnp.bfloat16)
    right_panel = lax.all_gather(right, "row", axis=0, tiled=True)
    selected = right_panel
    precond = lax.psum_scatter(
        lax.dot_general(
            selected, left_grad, (((1,), (1,)), ((), ())), preferred_element_type=jnp.float32
        ),
        "col",
        scatter_dimension=0,
        tiled=True,
    ).T
    new_weight = weight - 0.01 * precond
    narrow = new_weight.astype(jnp.bfloat16)
    spread = lax.all_to_all(tokens, "row", split_axis=1, concat_axis=0, tiled=True)
    selected = spread
    output = lax.psum_scatter(
        jnp.dot(selected, narrow, preferred_element_type=jnp.float32),
        "row",
        scatter_dimension=0,
        tiled=True,
    )
    return (new_weight, output.astype(jnp.bfloat16))


def solution(mesh):
    return jax.shard_map(
        shards,
        mesh=mesh,
        in_specs=(
            P("row", "col"),
            P("row", "col"),
            P("row", "col"),
            P("row", "col"),
            P("row", None),
        ),
        out_specs=(P("row", "col"), P("row", "col")),
        check_vma=False,
    )
```

profile of v0, /device:TPU:1, one launch (start us, length us, event | category | flops | bytes accessed | tf_op | source)
XLA Modules:
  0.0 570.2 jit_solution(13484413524477637766)
XLA Ops:
  7.2 0.0 all-gather.4.cloned.1.call-start
  7.2 0.7 all-gather.4.cloned.1.call-update
  7.9 0.0 all-gather.8.cloned.1.call-start
  7.9 0.7 all-gather.8.cloned.1.call-update
  8.6 0.0 all-gather.6.cloned.1.call-start
  8.7 0.7 all-gather.6.cloned.1.call-update
  9.4 0.0 reduce-scatter.3.cloned.1.call-start
  9.4 111.3 %all-gather.4.cloned.1.call-done = bf16[256,8192]{1,0:T(8,128)(2,1)} async-done(((bf16[256,1024]{1,0:T(8,128)(2,1)}), bf16[256,8192]{1,0:T(8,128)(2,1)}) %all-gather.4.cloned.1.call-update) | async-done | bytes 4194320 | tf_op jit(solution)/shard_map/all_gather | solution.py:8
  120.7 60.1 %all-gather.8.cloned.1.call-done = bf16[4096,512]{1,0:T(8,128)(2,1)} async-done(((bf16[128,512]{1,0:T(8,128)(2,1)}), bf16[4096,512]{1,0:T(8,128)(2,1)}) %all-gather.8.cloned.1.call-update) | async-done | bytes 4194320 | tf_op jit(solution)/shard_map/all_gather | solution.py:15
  180.9 69.8 %all-gather.6.cloned.1.call-done = bf16[8192,512]{1,0:T(8,128)(2,1)} async-done(((bf16[256,512]{1,0:T(8,128)(2,1)}), bf16[8192,512]{1,0:T(8,128)(2,1)}) %all-gather.6.cloned.1.call-update) | async-done | bytes 8388624 | tf_op jit(solution)/shard_map/all_gather | solution.py:11
  250.7 11.2 %convolution_bitcast_fusion.1 = f32[4096,256]{0,1:T(8,128)} fusion(bf16[4096,512]{1,0:T(8,128)(2,1)} %all-gather.8.cloned.1.call-done, bf16[256,8192]{1,0:T(8,128)(2,1)} %all-gather.4.cloned.1.call-done, bf16[8192,512]{1,0:T(8,128)(2,1)} %all-gather.6.cloned.1.call-done), kind=kOutput, calls=%fused_computation.1 | convolution fusion | flops 3221356544 | bytes 20971520 | tf_op jit(solution)/shard_map/dot_general | solution.py:18
  261.9 0.0 copy-start
  261.9 0.0 reduce-scatter.3.cloned.1.call-update
  262.0 0.0 reduce-scatter.5.cloned.1.call-start
  262.0 1.5 copy-done
  263.5 2.4 copy.9
  266.0 0.0 copy-start.2
  266.0 100.4 %all_to_all.19 = bf16[128,32,256]{0,2,1:T(8,128)(2,1)S(1)} all-to-all(bf16[128,32,256]{0,2,1:T(8,128)(2,1)} %bitcast.14), channel_id=1, replica_groups=mesh['row'=32,'col'=8] {'row'}, dimensions={1} | all-to-all | bytes 4194304 | tf_op jit(solution)/shard_map/all_to_all | solution.py:27
  366.4 2.9 copy.10
  369.3 27.2 %reduce-scatter.3.cloned.1.call-done = f32[512,256]{0,1:T(8,128)} async-done(((f32[4096,256]{0,1:T(8,128)}), f32[512,256]{0,1:T(8,128)}) %reduce-scatter.3.cloned.1.call-update) | async-done | bytes 524304 | tf_op jit(solution)/shard_map/reduce_scatter | solution.py:17
  396.5 0.0 copy-done.2
  396.5 1.1 bitcast_subtract_fusion
  397.7 0.0 copy-start.1
  397.7 6.3 %convolution_bitcast_fusion = f32[4096,512]{0,1:T(8,128)} fusion(bf16[4096,256]{1,0:T(8,128)(2,1)} %bitcast.15, f32[256,512]{1,0:T(8,128)S(1)} %bitcast_subtract_fusion), kind=kOutput, calls=%fused_computation | convolution fusion | flops 1073872896 | bytes 11010048 | tf_op jit(solution)/shard_map/dot_general | solution.py:30
  404.0 0.0 copy-done.1
  404.0 0.0 reduce-scatter.5.cloned.1.call-update
  404.0 157.9 %reduce-scatter.5.cloned.1.call-done = f32[128,512]{0,1:T(8,128)} async-done(((f32[4096,512]{0,1:T(8,128)}), f32[128,512]{0,1:T(8,128)}) %reduce-scatter.5.cloned.1.call-update) | async-done | bytes 262160 | tf_op jit(solution)/shard_map/reduce_scatter | solution.py:29
  561.9 1.0 convert_element_type.11
  562.9 0.8 copy.11
Async XLA Ops:
  7.2 113.6 %all-gather.4.cloned.1.call-start = ((), (), s32[]{:S(2)}) async-start(), calls=%async_computation.3 | async-start | bytes 4718592 | tf_op jit(solution)/shard_map/all_gather | solution.py:8
  7.9 173.0 %all-gather.8.cloned.1.call-start = ((), (), s32[]{:S(2)}) async-start(), calls=%async_computation.5 | async-start | bytes 4325376 | tf_op jit(solution)/shard_map/all_gather | solution.py:15
  8.6 242.1 %all-gather.6.cloned.1.call-start = ((), (), s32[]{:S(2)}) async-start(), calls=%async_computation.4 | async-start | bytes 8650752 | tf_op jit(solution)/shard_map/all_gather | solution.py:11
  9.4 387.2 %reduce-scatter.3.cloned.1.call-start = ((), (), s32[]{:S(2)}) async-start(), calls=%async_computation.6 | async-start | bytes 4718592 | tf_op jit(solution)/shard_map/reduce_scatter | solution.py:17
  261.9 1.6 copy-start
  262.0 300.0 %reduce-scatter.5.cloned.1.call-start = ((), (), s32[]{:S(2)}) async-start(), calls=%async_computation.7 | async-start | bytes 8650752 | tf_op jit(solution)/shard_map/reduce_scatter | solution.py:29
  266.0 130.6 %copy-start.2 = (f32[256,512]{1,0:T(8,128)S(1)}, f32[256,512]{1,0:T(8,128)}, u32[]{:S(2)}) copy-start(f32[256,512]{1,0:T(8,128)} %param.5) | copy-start | bytes 1572868
  397.7 6.3 %copy-start.1 = (f32[256,512]{1,0:T(8,128)}, f32[256,512]{1,0:T(8,128)S(1)}, u32[]{:S(2)}) copy-start(f32[256,512]{1,0:T(8,128)S(1)} %bitcast_subtract_fusion) | copy-start | bytes 1572868
Sparse Core Ops, SparseCore 0:
  10.6 110.0 all-gather.3
  122.6 58.2 all-gather.7
  182.7 67.9 all-gather.5
  262.1 134.4 reduce-scatter.2
  404.1 157.7 reduce-scatter.4
where the time goes:
time: 573 us; the launch traced here: 570 us
  waiting for transfers between devices  429 us (75%)
  blocking collectives  100 us (17%)
  matrix products  17.5 us (3%)
  between operations  13.8 us (2%)
  local copies, waits for them, and re-layouts  7.66 us (1%)
    reduce_scatter x1, waiting for transfers between devices, shards(): lax.psum_scatter(jnp.dot(selected, narrow, preferred_element_type=jnp.flo...  158 us
    all_gather x1, waiting for transfers between devices, shards(): left_panel = lax.all_gather(left, 'col', axis=1, tiled=True)  111 us
    all_to_all x1, blocking collectives, shards(): lax.all_to_all(tokens, 'row', split_axis=1, concat_axis=0, tiled=True)  100 us
    all_gather x1, waiting for transfers between devices, shards(): lax.all_gather(grad, 'row', axis=0, tiled=True)  69.8 us
    all_gather x1, waiting for transfers between devices, shards(): right_panel = lax.all_gather(right, 'row', axis=0, tiled=True)  60.1 us
    reduce_scatter x1, waiting for transfers between devices, shards(): lax.psum_scatter(lax.dot_general(selected, left_grad, (((1,), (1,)), ((),...  27.2 us
  transfers between devices with their start and end apart: 5, of which 5 were waited for; matrix products, arithmetic and copies ran while one was open for 1% of the time, Pallas kernels for 0%

commit v1 on v0

v1 whole, which is shorter than its diff:
```python
import jax
import jax.numpy as jnp
from jax import lax
from jax.experimental import pallas as pl
from jax.experimental.pallas import tpu as pltpu
from jax.sharding import PartitionSpec as P

MESH = pl.DeviceIdType.MESH
BF = jnp.bfloat16
F32 = jnp.float32


def kernel(w_hbm, g_hbm, l_hbm, r_hbm, t_hbm, nw_hbm, out_hbm,
           Gp, Rp, Lp, Xp, Np, Tv, Wv, Ov, acc,
           ld, sr, sg, sl, sx, sn, rr, rg, rl, rx, rn):
    row, col = lax.axis_index("row"), lax.axis_index("col")
    y, zl, c = row // 8, (row // 2) % 4, row % 2
    x, zh = col // 2, col % 2
    yp, ym, y2 = (y + 1) % 4, (y + 3) % 4, (y + 2) % 4
    xp, xm, x2 = (x + 1) % 4, (x + 3) % 4, (x + 2) % 4

    def rid(y_, z_, c_):
        return (y_ * 4 + z_) * 2 + c_

    def dev(y_=y, z_=zl, c_=c, x_=x, h_=zh):
        return (rid(y_, z_, c_), x_ * 2 + h_)

    D_yp, D_ym = dev(y_=yp), dev(y_=ym)
    D_xp, D_xm = dev(x_=xp), dev(x_=xm)
    D_sib, D_zh = dev(c_=1 - c), dev(h_=1 - zh)
    me = row

    loads = [
        pltpu.make_async_copy(r_hbm, Rp.at[me], ld.at[0]),
        pltpu.make_async_copy(g_hbm.at[pl.ds(0, 128)], Gp.at[col, 0], ld.at[1]),
        pltpu.make_async_copy(l_hbm.at[pl.ds(0, 128)], Lp.at[col, 0], ld.at[2]),
        pltpu.make_async_copy(l_hbm.at[pl.ds(128, 128)], Lp.at[col, 1], ld.at[3]),
        pltpu.make_async_copy(t_hbm, Tv, ld.at[4]),
        pltpu.make_async_copy(w_hbm, Wv, ld.at[5]),
        pltpu.make_async_copy(g_hbm.at[pl.ds(128, 128)], Gp.at[col, 1], ld.at[6]),
    ]
    for cp in loads:
        cp.start()

    bar = pltpu.get_barrier_semaphore()
    peers = [D_yp, D_ym, D_xp, D_xm, D_sib, D_zh,
             dev(z_=(zl + 1) % 4), dev(z_=(zl + 3) % 4)]
    for p in peers:
        pl.semaphore_signal(bar, inc=1, device_id=p, device_id_type=MESH)
    pl.semaphore_wait(bar, len(peers))

    pending = []

    def send(src, sems, n, rs, d, cond=None):
        cp = pltpu.make_async_remote_copy(
            src_ref=src, dst_ref=src, send_sem=sems.at[n], recv_sem=rs,
            device_id=d, device_id_type=MESH)
        if cond is None:
            cp.start()
        else:
            pl.when(cond)(cp.start)
        pending.append((cp, cond))

    def wait_recv(ref, rs):
        pltpu.make_async_remote_copy(
            src_ref=ref, dst_ref=ref, send_sem=rs, recv_sem=rs,
            device_id=D_sib, device_id_type=MESH).wait_recv()

    zorder = [zl, zl + 1 - 2 * (zl % 2), 2 - zl // 2, 3 - 3 * (zl // 2)]

    class Rho:
        def __init__(self, buf, rows, ss, rs):
            self.buf, self.half, self.ss, self.rs, self.n = buf, rows // 2, ss, rs, 0

        def put(self, i, d, h=None, cond=None):
            k = self.n
            self.n += 1
            if h is None:
                send(self.buf.at[i], self.ss, k, self.rs.at[0, i], d, cond)
            else:
                send(self.buf.at[i, pl.ds(h * self.half, self.half)],
                     self.ss, k, self.rs.at[h, i], d, cond)

        def got(self, i, h=None):
            if h is None:
                wait_recv(self.buf.at[i], self.rs.at[0, i])
            else:
                wait_recv(self.buf.at[i, pl.ds(h * self.half, self.half)], self.rs.at[h, i])

        def own(self):
            self.put(me, dev(z_=jnp.minimum(zl + 1, 3)), cond=zl < 3)
            self.put(me, dev(z_=jnp.maximum(zl - 1, 0)), cond=zl > 0)
            self.put(me, D_yp)
            self.put(me, D_ym)
            self.put(me, D_sib)

        def Z(self, j):
            zb = zorder[j]
            i = rid(y, zb, c)
            self.got(i)
            right = zb < zl
            step = jnp.where(right, 1, -1)
            ok = jnp.where(right, zl < 3, zl > 0)
            self.put(i, dev(z_=jnp.clip(zl + step, 0, 3)), cond=ok)
            self.put(i, D_yp)
            self.put(i, D_ym)
            self.put(i, D_sib)

        def Y(self, j):
            i = rid(ym, zorder[j], c)
            self.got(i)
            self.put(i, D_yp, h=0)
            self.put(i, D_sib)
            i = rid(yp, zorder[j], c)
            self.got(i)
            self.put(i, D_ym, h=1)
            self.put(i, D_sib)

        def Y2(self, j):
            i = rid(y2, zorder[j], c)
            self.got(i, 0)
            self.got(i, 1)
            self.put(i, D_sib)

        def S(self, yy):
            for j in range(4):
                self.got(rid(yy, zorder[j], 1 - c))

    class Gamma:
        def __init__(self, buf, ss, rs):
            self.buf, self.ss, self.rs, self.n = buf, ss, rs, 0

        def put(self, i, h, d):
            k = self.n
            self.n += 1
            send(self.buf.at[i, h], self.ss, k, self.rs.at[h, i], d)

        def got(self, i, h):
            wait_recv(self.buf.at[i, h], self.rs.at[h, i])

        def own_zh(self, h):
            self.put(col, h, D_zh)

        def own_x(self):
            for h in range(2):
                self.put(col, h, D_xp if h == 0 else D_xm)
                self.put(col, h, D_xm if h == 0 else D_xp)

        def partner(self, h):
            i = x * 2 + 1 - zh
            self.got(i, h)
            self.put(i, h, D_xp)
            self.put(i, h, D_xm)

        def ring(self, b):
            hb = zh if b == 0 else 1 - zh
            self.got(xm * 2 + hb, 0)
            self.put(xm * 2 + hb, 0, D_xp)
            self.got(xp * 2 + hb, 1)
            self.put(xp * 2 + hb, 1, D_xm)

        def rest(self, b):
            hb = zh if b == 0 else 1 - zh
            self.got(xm * 2 + hb, 1)
            self.got(xp * 2 + hb, 0)
            self.got(x2 * 2 + hb, 0)
            self.got(x2 * 2 + hb, 1)

    R = Rho(Rp, 128, sr, rr)
    X = Rho(Xp, 256, sx, rx)
    N = Rho(Np, 256, sn, rn)
    G = Gamma(Gp, sg, rg)
    L = Gamma(Lp, sl, rl)

    loads[0].wait()
    R.own()
    loads[1].wait()
    loads[6].wait()
    G.own_zh(0)
    G.own_zh(1)
    G.own_x()
    loads[2].wait()
    loads[3].wait()
    L.own_x()
    L.own_zh(0)
    R.Z(1)
    R.Y(0)
    G.ring(0)
    R.Z(2)
    R.Y(1)
    R.Y2(0)
    R.Z(3)
    R.Y(2)
    R.Y2(1)
    G.partner(0)
    G.partner(1)
    R.Y(3)
    R.Y2(2)
    G.ring(1)
    L.ring(0)
    R.Y2(3)
    for yy in (y, ym, yp, y2):
        R.S(yy)
    G.rest(0)
    G.rest(1)

    acc[...] = jnp.zeros_like(acc)

    @pl.loop(0, 8)
    def _(k):
        a = Gp[k].reshape(256, 512)
        b = Rp[pl.ds(4 * k, 4)].reshape(512, 512)
        acc[...] += jnp.dot(a, b, preferred_element_type=F32)

    Xp[me] = acc[...].astype(BF)
    X.own()
    L.own_zh(1)
    L.partner(0)
    X.Z(1)
    X.Y(0)
    X.Z(2)
    X.Y(1)
    X.Y2(0)
    X.Z(3)
    X.Y(2)
    X.Y2(1)
    X.Y(3)
    X.Y2(2)
    L.partner(1)
    L.ring(1)
    L.rest(0)
    L.rest(1)

    def gather_dot(lhs, rhs, yy):
        @pl.loop(0, 2)
        def _(i):
            k = 2 * yy + i
            acc[...] += jnp.dot(lhs[k].reshape(256, 1024),
                                rhs[pl.ds(4 * k, 4)].reshape(1024, 512),
                                preferred_element_type=F32)

    acc[...] = jnp.zeros_like(acc)
    X.S(y)
    gather_dot(Lp, Xp, y)
    X.S(ym)
    gather_dot(Lp, Xp, ym)
    X.S(yp)
    gather_dot(Lp, Xp, yp)
    X.Y2(3)
    X.S(y2)
    gather_dot(Lp, Xp, y2)

    loads[4].wait()
    loads[5].wait()
    nw = Wv[...] - 0.01 * acc[...]
    Np[me] = nw.astype(BF)
    N.own()
    Wv[...] = nw
    store_nw = pltpu.make_async_copy(Wv, nw_hbm, ld.at[6])
    store_nw.start()

    def out_dot(yy):
        @pl.loop(0, 2)
        def _(i):
            k = 2 * yy + i
            acc[pl.ds(0, 128)] += jnp.dot(
                Tv[:, pl.ds(pl.multiple_of(k * 1024, 1024), 1024)],
                Np[pl.ds(4 * k, 4)].reshape(1024, 512),
                preferred_element_type=F32)

    acc[...] = jnp.zeros_like(acc)
    N.Z(1)
    N.Y(0)
    N.Z(2)
    N.Y(1)
    N.Y2(0)
    N.Z(3)
    N.Y(2)
    N.Y2(1)
    N.Y(3)
    N.Y2(2)
    N.S(y)
    out_dot(y)
    N.S(ym)
    out_dot(ym)
    N.S(yp)
    out_dot(yp)
    N.Y2(3)
    N.S(y2)
    out_dot(y2)
    Ov[...] = acc[pl.ds(0, 128)].astype(BF)
    store_out = pltpu.make_async_copy(Ov, out_hbm, ld.at[7])
    store_out.start()
    for cp, cond in pending:
        if cond is None:
            cp.wait_send()
        else:
            pl.when(cond)(cp.wait_send)
    store_nw.wait()
    store_out.wait()


def shards(weight, grad, left, right, tokens):
    any_ = pl.BlockSpec(memory_space=pl.ANY)
    dma = pltpu.SemaphoreType.DMA
    return pl.pallas_call(
        kernel,
        out_shape=(jax.ShapeDtypeStruct((256, 512), F32), jax.ShapeDtypeStruct((128, 512), BF)),
        in_specs=[any_] * 5,
        out_specs=(any_, any_),
        scratch_shapes=[
            pltpu.VMEM((8, 2, 128, 512), BF),
            pltpu.VMEM((32, 128, 512), BF),
            pltpu.VMEM((8, 2, 128, 1024), BF),
            pltpu.VMEM((32, 256, 512), BF),
            pltpu.VMEM((32, 256, 512), BF),
            pltpu.VMEM((128, 8192), BF),
            pltpu.VMEM((256, 512), F32),
            pltpu.VMEM((128, 512), BF),
            pltpu.VMEM((256, 512), F32),
            dma((8,)), dma((40,)), dma((16,)), dma((16,)), dma((40,)), dma((40,)),
            dma((2, 32)), dma((2, 8)), dma((2, 8)), dma((2, 32)), dma((2, 32)),
        ],
        compiler_params=pltpu.CompilerParams(
            collective_id=0, has_side_effects=True, vmem_limit_bytes=56 * 2**20),
    )(weight, grad, left, right, tokens)


def solution(mesh):
    return jax.shard_map(
        shards,
        mesh=mesh,
        in_specs=(
            P("row", "col"),
            P("row", "col"),
            P("row", "col"),
            P("row", "col"),
            P("row", None),
        ),
        out_specs=(P("row", "col"), P("row", "col")),
        check_vma=False,
    )
```

time: 573 us -> 169 us (0.29)
  waiting for transfers between devices: 429 us -> 0 us
  Pallas kernels: 0 us -> 165 us
  blocking collectives: 100 us -> 0 us
  matrix products: 17.5 us -> 0 us
  between operations: 13.8 us -> 0.64 us
    all_gather x3 -> x0, waiting for transfers between devices: 241 us -> none  [the longest x1 111 us: shards(): left_panel = lax.all_gather(left, 'col', axis=1, tiled=True)]
    reduce_scatter x2 -> x0, waiting for transfers between devices: 185 us -> none  [the longest x1 158 us: shards(): lax.psum_scatter(jnp.dot(selected, narrow, preferred_element_type=jnp.flo...]
    pallas_call x0 -> x1, Pallas kernels: none -> 165 us  [shards(): pl.pallas_call(kernel, out_shape=(jax.ShapeDtypeStruct((256, 512), F32),...]
    all_to_all x1 -> x0, blocking collectives: 100 us -> none  [shards(): lax.all_to_all(tokens, 'row', split_axis=1, concat_axis=0, tiled=True)]
    dot_general x2 -> x0, matrix products: 17.5 us -> none  [the longest x1 11.2 us: shards(): lax.dot_general(selected, left_grad, (((1,), (1,)), ((), ())), preferred_...]
  transfers between devices with their start and end apart: 5 -> 0, of which waited for: 5 -> 0; matrix products, arithmetic and copies ran while one was open for 1% -> 0% of each run, Pallas kernels for 0% -> 0%
where the time goes in v1:
time: 169 us
  Pallas kernels  165 us (98%)
  local copies, waits for them, and re-layouts  3.44 us (2%)
    pallas_call x1, Pallas kernels, shards(): pl.pallas_call(kernel, out_shape=(jax.ShapeDtypeStruct((256, 512), F32),...  165 us
    unnamed x2, local copies, waits for them, and re-layouts  3.44 us

profile of v1, /device:TPU:1, one launch (start us, length us, event | category | flops | bytes accessed | tf_op | source)
XLA Modules:
  0.0 169.1 jit_solution(13277383174454924967)
XLA Ops:
  0.6 165.0 %shard_map.68 = (f32[256,512]{1,0:T(8,128)}, bf16[128,512]{1,0:T(8,128)(2,1)}) custom-call(f32[256,512]{1,0:T(8,128)} %w_hbm.1, bf16[256,512]{1,0:T(8,128)(2,1)} %g_hbm.1, bf16[256,1024]{1,0:T(8,128)(2,1)} %l_hbm.1, bf16[128,512]{1,0:T(8,128)(2,1)} %r_hbm.1, bf16[128,8192]{1,0:T(8,128)(2,1)} %t_hbm.1), custom_call_target="tpu_custom_call" | custom-call | tf_op jit(solution)/shard_map/pallas_call | solution.py:306
  165.6 1.9 %copy.9 = f32[256,512]{1,0:T(8,128)} copy(f32[256,512]{1,0:T(8,128)} %get-tuple-element.4) | data formatting | bytes 1048576
  167.5 1.6 copy.10

commit v2 on v1

v2 whole, which is shorter than its diff:
```python
import jax
import jax.numpy as jnp
from jax import lax
from jax.experimental import pallas as pl
from jax.experimental.pallas import tpu as pltpu
from jax.sharding import PartitionSpec as P

MESH = pl.DeviceIdType.MESH
BF = jnp.bfloat16
F32 = jnp.float32


def kernel(w_hbm, g_hbm, l_hbm, r_hbm, t_hbm, nw_hbm, out_hbm,
           Gp, Rp, Lp, Xp, Np, Tq, Wv, Ov, acc, oacc, Ob, Ib,
           ld, sr, sg, sl, sx, sn, st, so, rr, rg, rl, rx, rn, rt, ro):
    row, col = lax.axis_index("row"), lax.axis_index("col")
    y, zl, c = row // 8, (row // 2) % 4, row % 2
    x, zh = col // 2, col % 2
    yp, ym, y2 = (y + 1) % 4, (y + 3) % 4, (y + 2) % 4
    xp, xm, x2 = (x + 1) % 4, (x + 3) % 4, (x + 2) % 4

    def rid(y_, z_, c_):
        return (y_ * 4 + z_) * 2 + c_

    def dev(y_=y, z_=zl, c_=c, x_=x, h_=zh):
        return (rid(y_, z_, c_), x_ * 2 + h_)

    D_yp, D_ym = dev(y_=yp), dev(y_=ym)
    D_xp, D_xm = dev(x_=xp), dev(x_=xm)
    D_sib, D_zh = dev(c_=1 - c), dev(h_=1 - zh)
    D_zr, D_zl = dev(z_=jnp.minimum(zl + 1, 3)), dev(z_=jnp.maximum(zl - 1, 0))
    me = row

    loads = [
        pltpu.make_async_copy(r_hbm, Rp.at[me], ld.at[0]),
        pltpu.make_async_copy(g_hbm.at[pl.ds(0, 128)], Gp.at[col, 0], ld.at[1]),
        pltpu.make_async_copy(w_hbm, Wv, ld.at[5]),
        pltpu.make_async_copy(g_hbm.at[pl.ds(128, 128)], Gp.at[col, 1], ld.at[4]),
    ]
    for cp in loads:
        cp.start()
    lloads = [pltpu.make_async_copy(l_hbm.at[pl.ds(64 * q, 64)], Lp.at[col, q], ld.at[12 + q])
              for q in range(4)]
    for cp in lloads:
        cp.start()
    tcols = pl.ds(pl.multiple_of(2048 * y, 2048), 2048)
    tloads = [pltpu.make_async_copy(t_hbm.at[pl.ds(32 * q, 32), tcols], Tq.at[q, y], ld.at[8 + q])
              for q in range(4)]
    for cp in tloads:
        cp.start()

    bar = pltpu.get_barrier_semaphore()
    D_y2, D_x2 = dev(y_=y2), dev(x_=x2)
    peers = [D_yp, D_ym, D_xp, D_xm, D_sib, D_zh, D_y2, D_x2,
             dev(z_=(zl + 1) % 4), dev(z_=(zl + 3) % 4)]
    for p in peers:
        pl.semaphore_signal(bar, inc=1, device_id=p, device_id_type=MESH)
    pl.semaphore_wait(bar, len(peers))

    pending = []

    def send(src, sems, n, rs, d, cond=None):
        cp = pltpu.make_async_remote_copy(
            src_ref=src, dst_ref=src, send_sem=sems.at[n], recv_sem=rs,
            device_id=d, device_id_type=MESH)
        if cond is None:
            cp.start()
        else:
            pl.when(cond)(cp.start)
        pending.append((src, sems.at[n], cond))

    def wait_recv(ref, rs):
        pltpu.make_async_remote_copy(
            src_ref=ref, dst_ref=ref, send_sem=rs, recv_sem=rs,
            device_id=D_sib, device_id_type=MESH).wait_recv()

    zorder = [zl, 1 + zl % 2, (2 + 3 * zl) % 5, 3 - 3 * (zl // 2)]

    zinfo = []
    for zb in zorder:
        right = zb < zl
        zinfo.append((zb, jnp.where(right, zl < 3, zl > 0),
                      dev(z_=jnp.clip(zl + jnp.where(right, 1, -1), 0, 3))))

    class Rho:
        def __init__(self, buf, rows, ss, rs):
            self.buf, self.half, self.ss, self.rs = buf, rows // 2, ss, rs
            self.keys, self.done = {}, set()

        def at(self, i, h):
            return self.buf.at[i, pl.ds(h * self.half, self.half)]

        def send(self, key, src, rs, d, cond=None):
            k = self.keys.setdefault(key, len(self.keys))
            cp = pltpu.make_async_remote_copy(
                src_ref=src, dst_ref=src, send_sem=self.ss.at[k], recv_sem=rs,
                device_id=d, device_id_type=MESH)
            if cond is None:
                cp.start()
            else:
                pl.when(cond)(cp.start)
            if key not in self.done:
                self.done.add(key)
                pending.append(((self.buf, None if key[1] == "s" else self.half), (self.ss, k), cond))

        def put(self, key, i, h, d, cond=None):
            self.send((key, h), self.at(i, h), self.rs.at[h, i], d, cond)

        def sib(self, key, i):
            self.send((key, "s"), self.buf.at[i], self.rs.at[0, i], D_sib)

        def got(self, i, h):
            wait_recv(self.at(i, h), self.rs.at[h, i])

        def own(self):
            for h in range(2):
                self.put("or", me, h, D_zr, zl < 3)
                self.put("ol", me, h, D_zl, zl > 0)
                self.put("oa", me, h, D_yp if h == 0 else D_ym)
                self.put("ob", me, h, D_ym if h == 0 else D_yp)
            self.sib("o", me)

        def zpart(self, j, h):
            zb, ok, d = zinfo[j]
            i = rid(y, zb, c)
            self.got(i, h)
            self.put(("z", j), i, h, d, ok)
            self.put(("za", j), i, h, D_yp if h == 0 else D_ym)
            self.put(("zb", j), i, h, D_ym if h == 0 else D_yp)

        def zsib(self, j):
            self.sib(("z", j), rid(y, zorder[j], c))

        def Z(self, j):
            self.zpart(j, 0)
            self.zpart(j, 1)
            self.zsib(j)

        def Z12(self):
            self.zpart(1, 0)
            self.zpart(2, 0)
            self.zpart(1, 1)
            self.zpart(2, 1)
            self.zsib(1)
            self.zsib(2)

        def Y(self, j):
            a, b = rid(ym, zorder[j], c), rid(yp, zorder[j], c)
            self.got(a, 0)
            self.put(("ya", j), a, 0, D_yp)
            self.got(b, 1)
            self.put(("yb", j), b, 1, D_ym)
            self.got(a, 1)
            self.sib(("ya", j), a)
            self.got(b, 0)
            self.sib(("yb", j), b)

        def Y2(self, j):
            i = rid(y2, zorder[j], c)
            self.got(i, 0)
            self.got(i, 1)
            self.sib(("y2", j), i)

        def zy(self):
            mid = (zl + 1) // 2 == 1

            @pl.when(mid)
            def _():
                self.Z12()
                self.Y(0)
                self.Z(3)

            @pl.when(jnp.logical_not(mid))
            def _():
                self.Z(1)
                self.Y(0)
                self.Z(2)
                self.Z(3)

        def S(self, yy):
            for j in range(4):
                i = rid(yy, zorder[j], 1 - c)
                wait_recv(self.buf.at[i], self.rs.at[0, i])

    class Gamma:
        def __init__(self, buf, ss, rs, parts):
            self.buf, self.ss, self.rs, self.parts, self.n = buf, ss, rs, parts, 0

        def put(self, i, p, d):
            send(self.buf.at[i, p], self.ss, self.n, self.rs.at[p, i], d)
            self.n += 1

        def got(self, i, p):
            wait_recv(self.buf.at[i, p], self.rs.at[p, i])

        def own_zh(self, p):
            self.put(col, p, D_zh)

        def own_x(self, p):
            self.put(col, p, D_xp if p % 2 == 0 else D_xm)
            self.put(col, p, D_xm if p % 2 == 0 else D_xp)

        def partner(self, p):
            i = x * 2 + 1 - zh
            self.got(i, p)
            self.put(i, p, D_xp if p % 2 == 0 else D_xm)
            self.put(i, p, D_xm if p % 2 == 0 else D_xp)

        def ring(self, b, p):
            hb = zh if b == 0 else 1 - zh
            if p % 2 == 0:
                self.got(xm * 2 + hb, p)
                self.put(xm * 2 + hb, p, D_xp)
            else:
                self.got(xp * 2 + hb, p)
                self.put(xp * 2 + hb, p, D_xm)

        def rest(self, b, p):
            hb = zh if b == 0 else 1 - zh
            self.got((xp if p % 2 == 0 else xm) * 2 + hb, p)
            self.got(x2 * 2 + hb, p)


    class Tok:
        n = 0

        def own_y(self):
            for q, d in ((yp, D_yp), (ym, D_ym), (y2, D_y2)):
                cp = pltpu.make_async_remote_copy(
                    src_ref=t_hbm.at[pl.ds(pl.multiple_of(32 * x, 32), 32),
                                     pl.ds(pl.multiple_of(2048 * q, 2048), 2048)],
                    dst_ref=Tq.at[x, y], send_sem=st.at[self.n], recv_sem=rt.at[x, y],
                    device_id=d, device_id_type=MESH)
                cp.start()
                self.n += 1
                pending.append((cp.src_ref, cp.src_sem, None))

        def share_x(self, q):
            if True:
                wait_recv(Tq.at[x, q], rt.at[x, q])
                for d in (D_xp, D_xm, D_x2):
                    send(Tq.at[x, q], st, self.n, rt.at[x, q], d)
                    self.n += 1

        def rest(self):
            for xx in (xp, xm, x2):
                for q in (yp, ym, y2):
                    wait_recv(Tq.at[xx, q], rt.at[xx, q])

    class Nar:
        n = 0

        def put(self, i, h, d, cond=None):
            send(Np.at[i, pl.ds(128 * h, 128)], sn, self.n, rn.at[h, i], d, cond)
            self.n += 1

        def sib(self, i):
            send(Np.at[i], sn, self.n, rn.at[0, i], D_sib)
            self.n += 1

        def own(self):
            i = 2 * zl + c
            for h in range(2):
                self.put(i, h, D_zr, zl < 3)
                self.put(i, h, D_zl, zl > 0)
            self.sib(i)

        def zpart(self, j, h):
            zb, ok, d = zinfo[j]
            i = 2 * zb + c
            wait_recv(Np.at[i, pl.ds(128 * h, 128)], rn.at[h, i])
            self.put(i, h, d, ok)

        def Z12(self):
            for h in range(2):
                self.zpart(1, h)
                self.zpart(2, h)
            self.sib(2 * zorder[1] + c)
            self.sib(2 * zorder[2] + c)

        def Z3(self):
            self.zpart(3, 0)
            self.zpart(3, 1)
            self.sib(2 * zorder[3] + c)

        def S(self, j):
            i = 2 * zorder[j] + 1 - c
            wait_recv(Np.at[i], rn.at[0, i])

    R = Rho(Rp, 128, sr, rr)
    X = Rho(Xp, 256, sx, rx)
    N = Nar()
    T = Tok()
    G = Gamma(Gp, sg, rg, 2)
    L = Gamma(Lp, sl, rl, 4)


    def x_dot(k):
        acc[...] += jnp.dot(Gp[k].reshape(256, 512), Rp[pl.ds(4 * k, 4)].reshape(512, 512),
                            preferred_element_type=F32)

    def x_half(hb):
        @pl.loop(0, 4)
        def _(q):
            x_dot(2 * q + hb)

    acc[...] = jnp.zeros_like(acc)
    loads[0].wait()
    loads[1].wait()
    loads[3].wait()
    G.own_zh(0)
    R.own()
    G.own_x(0)
    G.own_x(1)
    G.partner(0)
    R.zy()
    for cp in lloads: cp.wait()
    G.own_zh(1)
    G.ring(0, 0)
    G.ring(0, 1)
    L.own_x(0)
    L.own_x(1)
    L.own_zh(0)
    L.own_zh(1)
    R.Y(1)
    R.Y2(0)
    G.ring(1, 0)
    R.Y(2)
    R.Y2(1)
    G.partner(1)
    R.Y(3)
    T.own_y()
    R.Y2(2)
    R.Y2(3)
    G.ring(1, 1)
    L.own_x(2)
    L.own_x(3)
    L.ring(0, 0)
    L.ring(0, 1)
    R.S(y)
    R.S(ym)
    R.S(yp)
    R.S(y2)
    G.rest(0, 0)
    G.rest(0, 1)
    x_half(zh)
    G.rest(1, 0)
    G.rest(1, 1)
    x_half(1 - zh)
    Xp[me] = acc[...].astype(BF)
    X.own()
    L.partner(0)
    L.ring(0, 2)
    L.ring(0, 3)
    L.partner(1)
    T.share_x(yp)
    X.zy()
    L.own_zh(2)
    L.own_zh(3)
    X.Y(1)
    L.ring(1, 0)
    L.ring(1, 1)
    X.Y2(0)
    X.Y(2)
    L.partner(2)
    X.Y2(1)
    X.Y(3)
    L.partner(3)
    L.ring(1, 2)
    X.Y2(2)
    X.Y2(3)
    L.ring(1, 3)
    T.share_x(ym)
    T.share_x(y2)
    for b in range(8): L.rest(b // 4, b % 4)

    def gather_dot(lhs, rhs, yy):
        @pl.loop(0, 2)
        def _(i):
            k = 2 * yy + i
            acc[...] += jnp.dot(lhs[k].reshape(256, 1024),
                                rhs[pl.ds(4 * k, 4)].reshape(1024, 512),
                                preferred_element_type=F32)

    acc[...] = jnp.zeros_like(acc)
    X.S(y)
    gather_dot(Lp, Xp, y)
    X.S(ym)
    gather_dot(Lp, Xp, ym)
    X.S(yp)
    gather_dot(Lp, Xp, yp)
    X.S(y2)
    gather_dot(Lp, Xp, y2)

    loads[2].wait()
    nw = Wv[...] - 0.01 * acc[...]
    Np[2 * zl + c] = nw.astype(BF)
    N.own()
    Wv[...] = nw
    store_nw = pltpu.make_async_copy(Wv, nw_hbm, ld.at[6])
    store_nw.start()

    def out_dot(j, first):
        zb = zorder[j]
        lhs = Tq[:, :, :, pl.ds(pl.multiple_of(512 * zb, 512), 512)].reshape(512, 512)
        v = jnp.dot(lhs, Np[pl.ds(2 * zb, 2)].reshape(512, 512), preferred_element_type=F32)
        if first:
            oacc[...] = v
        else:
            oacc[...] += v

    for cp in tloads:
        cp.wait()
    N.Z12()
    T.rest()
    N.S(0)
    out_dot(0, True)
    N.S(1)
    out_dot(1, False)
    N.S(2)
    out_dot(2, False)
    N.Z3()
    N.S(3)
    out_dot(3, False)
    part = oacc[...].reshape(4, 4, 32, 512)
    for q in range(4):
        Ob[q] = part[:, q].reshape(128, 512).astype(BF)
    for k, (q, d) in enumerate(((yp, D_yp), (ym, D_ym), (y2, D_y2))):
        cp = pltpu.make_async_remote_copy(
            src_ref=Ob.at[q], dst_ref=Ib.at[y], send_sem=so.at[k], recv_sem=ro.at[y],
            device_id=d, device_id_type=MESH)
        cp.start()
        pending.append((cp.src_ref, cp.src_sem, None))
    for q in range(4):
        @pl.when(q == y)
        def _(q=q):
            acc[pl.ds(0, 128)] = oacc[...].reshape(4, 4, 32, 512)[:, q].reshape(128, 512)
    for q in (yp, ym, y2):
      wait_recv(Ib.at[q], ro.at[q])
    Ov[...] = (acc[pl.ds(0, 128)] + Ib[yp].astype(F32) + Ib[ym].astype(F32)
               + Ib[y2].astype(F32)).astype(BF)
    store_out = pltpu.make_async_copy(Ov, out_hbm, ld.at[7])
    store_out.start()
    for src, sem, cond in pending:
        if isinstance(src, tuple):
            src = src[0].at[0] if src[1] is None else src[0].at[0, pl.ds(0, src[1])]
            sem = sem[0].at[sem[1]]
        cp = pltpu.make_async_remote_copy(
            src_ref=src, dst_ref=src, send_sem=sem, recv_sem=sem,
            device_id=D_sib, device_id_type=MESH)
        if cond is None:
            cp.wait_send()
        else:
            pl.when(cond)(cp.wait_send)
    store_nw.wait()
    store_out.wait()


def shards(weight, grad, left, right, tokens):
    any_ = pl.BlockSpec(memory_space=pl.ANY)
    dma = pltpu.SemaphoreType.DMA
    return pl.pallas_call(
        kernel,
        out_shape=(jax.ShapeDtypeStruct((256, 512), F32), jax.ShapeDtypeStruct((128, 512), BF)),
        in_specs=[any_] * 5,
        out_specs=(any_, any_),
        scratch_shapes=[
            pltpu.VMEM((8, 2, 128, 512), BF),
            pltpu.VMEM((32, 128, 512), BF),
            pltpu.VMEM((8, 4, 64, 1024), BF),
            pltpu.VMEM((32, 256, 512), BF),
            pltpu.VMEM((8, 256, 512), BF),
            pltpu.VMEM((4, 4, 32, 2048), BF),
            pltpu.VMEM((256, 512), F32),
            pltpu.VMEM((128, 512), BF),
            pltpu.VMEM((256, 512), F32),
            pltpu.VMEM((512, 512), F32),
            pltpu.VMEM((4, 128, 512), BF),
            pltpu.VMEM((4, 128, 512), BF),
            dma((16,)), dma((52,)), dma((16,)), dma((28,)), dma((52,)), dma((20,)), dma((12,)), dma((4,)),
            dma((2, 32)), dma((2, 8)), dma((4, 8)), dma((2, 32)), dma((2, 8)), dma((4, 4)), dma((4,)),
        ],
        compiler_params=pltpu.CompilerParams(
            collective_id=0, has_side_effects=True, vmem_limit_bytes=56 * 2**20),
    )(weight, grad, left, right, tokens)


def solution(mesh):
    return jax.shard_map(
        shards,
        mesh=mesh,
        in_specs=(
            P("row", "col"),
            P("row", "col"),
            P("row", "col"),
            P("row", "col"),
            P("row", None),
        ),
        out_specs=(P("row", "col"), P("row", "col")),
        check_vma=False,
    )
```

time: 169 us -> 130 us (0.77)
  Pallas kernels: 165 us -> 126 us
    pallas_call x1, Pallas kernels: 165 us -> 126 us  [shards(): pl.pallas_call(kernel, out_shape=(jax.ShapeDtypeStruct((256, 512), F32),...]
where the time goes in v2:
time: 130 us
  Pallas kernels  126 us (97%)
  local copies, waits for them, and re-layouts  3.44 us (3%)
    pallas_call x1, Pallas kernels, shards(): pl.pallas_call(kernel, out_shape=(jax.ShapeDtypeStruct((256, 512), F32),...  126 us
    unnamed x2, local copies, waits for them, and re-layouts  3.44 us

profile of v2, /device:TPU:1, one launch (start us, length us, event | category | flops | bytes accessed | tf_op | source)
XLA Modules:
  0.0 130.1 jit_solution(4822996824717664664)
XLA Ops:
  0.6 126.0 %shard_map.68 = (f32[256,512]{1,0:T(8,128)}, bf16[128,512]{1,0:T(8,128)(2,1)}) custom-call(f32[256,512]{1,0:T(8,128)} %w_hbm.1, bf16[256,512]{1,0:T(8,128)(2,1)} %g_hbm.1, bf16[256,1024]{1,0:T(8,128)(2,1)} %l_hbm.1, bf16[128,512]{1,0:T(8,128)(2,1)} %r_hbm.1, bf16[128,8192]{1,0:T(8,128)(2,1)} %t_hbm.1), custom_call_target="tpu_custom_call" | custom-call | tf_op jit(solution)/shard_map/pallas_call | solution.py:462
  126.6 1.9 %copy.9 = f32[256,512]{1,0:T(8,128)} copy(f32[256,512]{1,0:T(8,128)} %get-tuple-element.4) | data formatting | bytes 1048576
  128.5 1.6 %copy.10 = bf16[128,512]{1,0:T(8,128)(2,1)} copy(bf16[128,512]{1,0:T(8,128)(2,1)} %get-tuple-element.5) | data formatting | bytes 262144

commit v3 on v2

--- a/solution.py
+++ b/solution.py
@@ -112,13 +112,14 @@
         def got(self, i, h):
             wait_recv(self.at(i, h), self.rs.at[h, i])
 
-        def own(self):
-            for h in range(2):
+        def own(self, hs=None):
+            for h in (range(2) if hs is None else (hs,)):
                 self.put("or", me, h, D_zr, zl < 3)
                 self.put("ol", me, h, D_zl, zl > 0)
                 self.put("oa", me, h, D_yp if h == 0 else D_ym)
                 self.put("ob", me, h, D_ym if h == 0 else D_yp)
-            self.sib("o", me)
+            if hs != 0:
+                self.sib("o", me)
 
         def zpart(self, j, h):
             zb, ok, d = zinfo[j]
@@ -175,7 +176,14 @@
                 self.Z(1)
                 self.Y(0)
                 self.Z(2)
+                self.Y(1)
                 self.Z(3)
+
+        def y1(self):
+            @pl.when((zl + 1) // 2 == 1)
+            def _():
+                self.Y(1)
+
 
         def S(self, yy):
             for j in range(4):
@@ -224,28 +232,28 @@
     class Tok:
         n = 0
 
-        def own_y(self):
-            for q, d in ((yp, D_yp), (ym, D_ym), (y2, D_y2)):
-                cp = pltpu.make_async_remote_copy(
-                    src_ref=t_hbm.at[pl.ds(pl.multiple_of(32 * x, 32), 32),
-                                     pl.ds(pl.multiple_of(2048 * q, 2048), 2048)],
-                    dst_ref=Tq.at[x, y], send_sem=st.at[self.n], recv_sem=rt.at[x, y],
-                    device_id=d, device_id_type=MESH)
-                cp.start()
+        def own_y(self, r):
+            if True:
+                for q, d in ((yp, D_yp), (ym, D_ym), (y2, D_y2)):
+                    cp = pltpu.make_async_remote_copy(
+                        src_ref=t_hbm.at[pl.ds(pl.multiple_of(32 * r, 32), 32),
+                                         pl.ds(pl.multiple_of(2048 * q, 2048), 2048)],
+                        dst_ref=Tq.at[r, y], send_sem=st.at[self.n], recv_sem=rt.at[r, y],
+                        device_id=d, device_id_type=MESH)
+                    cp.start()
+                    self.n += 1
+                    pending.append((cp.src_ref, cp.src_sem, None))
+
+        def share_x(self, q):
+            wait_recv(Tq.at[x, q], rt.at[x, q])
+            for d in (D_xp, D_xm):
+                send(Tq.at[x, q], st, self.n, rt.at[x, q], d)
                 self.n += 1
-                pending.append((cp.src_ref, cp.src_sem, None))
-
-        def share_x(self, q):
-            if True:
-                wait_recv(Tq.at[x, q], rt.at[x, q])
-                for d in (D_xp, D_xm, D_x2):
-                    send(Tq.at[x, q], st, self.n, rt.at[x, q], d)
-                    self.n += 1
 
         def rest(self):
-            for xx in (xp, xm, x2):
+            for r in (xp, xm, x2):
                 for q in (yp, ym, y2):
-                    wait_recv(Tq.at[xx, q], rt.at[xx, q])
+                    wait_recv(Tq.at[r, q], rt.at[r, q])
 
     class Nar:
         n = 0
@@ -258,12 +266,12 @@
             send(Np.at[i], sn, self.n, rn.at[0, i], D_sib)
             self.n += 1
 
-        def own(self):
+        def own(self, h):
             i = 2 * zl + c
-            for h in range(2):
-                self.put(i, h, D_zr, zl < 3)
-                self.put(i, h, D_zl, zl > 0)
-            self.sib(i)
+            self.put(i, h, D_zr, zl < 3)
+            self.put(i, h, D_zl, zl > 0)
+            if h == 1:
+                self.sib(i)
 
         def zpart(self, j, h):
             zb, ok, d = zinfo[j]
@@ -295,14 +303,46 @@
     L = Gamma(Lp, sl, rl, 4)
 
 
-    def x_dot(k):
-        acc[...] += jnp.dot(Gp[k].reshape(256, 512), Rp[pl.ds(4 * k, 4)].reshape(512, 512),
-                            preferred_element_type=F32)
-
-    def x_half(hb):
+    def x_part(h, hb):
         @pl.loop(0, 4)
         def _(q):
-            x_dot(2 * q + hb)
+            k = 2 * q + hb
+            acc[pl.ds(128 * h, 128)] += jnp.dot(
+                Gp[k, h], Rp[pl.ds(4 * k, 4)].reshape(512, 512), preferred_element_type=F32)
+
+    def x_done(h):
+        Xp[me, pl.ds(128 * h, 128)] = acc[pl.ds(128 * h, 128)].astype(BF)
+        acc[pl.ds(128 * h, 128)] = jnp.zeros((128, 512), F32)
+        X.own(h)
+
+    def p(h, yy):
+        @pl.loop(0, 2)
+        def _(i):
+            k = 2 * yy + i
+            acc[pl.ds(128 * h, 128)] += jnp.dot(
+                Lp[k, pl.ds(2 * h, 2)].reshape(128, 1024),
+                Xp[pl.ds(4 * k, 4)].reshape(1024, 512), preferred_element_type=F32)
+
+    stores = []
+
+    def finish_rows(h):
+        rows = pl.ds(128 * h, 128)
+        nw = Wv[rows] - 0.01 * acc[rows]
+        Np[2 * zl + c, rows] = nw.astype(BF)
+        N.own(h)
+        Wv[rows] = nw
+        cp = pltpu.make_async_copy(Wv.at[rows], nw_hbm.at[rows], ld.at[6 + h])
+        cp.start()
+        stores.append(cp)
+
+    def out_dot(j, first):
+        zb = zorder[j]
+        lhs = Tq[:, :, :, pl.ds(pl.multiple_of(512 * zb, 512), 512)].reshape(512, 512)
+        v = jnp.dot(lhs, Np[pl.ds(2 * zb, 2)].reshape(512, 512), preferred_element_type=F32)
+        if first:
+            oacc[...] = v
+        else:
+            oacc[...] += v
 
     acc[...] = jnp.zeros_like(acc)
     loads[0].wait()
@@ -312,105 +352,93 @@
     R.own()
     G.own_x(0)
     G.own_x(1)
+    T.own_y(x)
     G.partner(0)
     R.zy()
     for cp in lloads: cp.wait()
     G.own_zh(1)
     G.ring(0, 0)
     G.ring(0, 1)
+    R.y1()
+    R.Y2(0)
+    G.ring(1, 0)
     L.own_x(0)
     L.own_x(1)
+    R.Y(2)
+    R.Y2(1)
+    R.Y(3)
+    R.Y2(2)
+    G.partner(1)
     L.own_zh(0)
     L.own_zh(1)
-    R.Y(1)
-    R.Y2(0)
-    G.ring(1, 0)
-    R.Y(2)
-    R.Y2(1)
-    G.partner(1)
-    R.Y(3)
-    T.own_y()
-    R.Y2(2)
     R.Y2(3)
-    G.ring(1, 1)
-    L.own_x(2)
-    L.own_x(3)
-    L.ring(0, 0)
-    L.ring(0, 1)
     R.S(y)
     R.S(ym)
     R.S(yp)
     R.S(y2)
     G.rest(0, 0)
+    G.rest(1, 0)
+    G.ring(1, 1)
+    x_part(0, zh)
+    x_part(0, 1 - zh)
+    x_done(0)
     G.rest(0, 1)
-    x_half(zh)
-    G.rest(1, 0)
+    x_part(1, zh)
     G.rest(1, 1)
-    x_half(1 - zh)
-    Xp[me] = acc[...].astype(BF)
-    X.own()
+    x_part(1, 1 - zh)
+    x_done(1)
+    L.own_x(2)
+    L.own_x(3)
+    L.ring(0, 0)
+    L.ring(0, 1)
     L.partner(0)
+    X.zy()
+    L.own_zh(2)
+    L.partner(1)
     L.ring(0, 2)
     L.ring(0, 3)
-    L.partner(1)
-    T.share_x(yp)
-    X.zy()
-    L.own_zh(2)
-    L.own_zh(3)
-    X.Y(1)
+    X.y1()
     L.ring(1, 0)
     L.ring(1, 1)
     X.Y2(0)
+    L.own_zh(3)
+    L.partner(2)
     X.Y(2)
-    L.partner(2)
     X.Y2(1)
     X.Y(3)
+    L.ring(1, 2)
+    L.rest(0, 0)
+    L.rest(0, 1)
+    L.rest(1, 0)
+    L.rest(1, 1)
     L.partner(3)
-    L.ring(1, 2)
+    X.S(y)
+    p(0, y)
+    X.S(ym)
+    p(0, ym)
     X.Y2(2)
+    X.S(yp)
+    p(0, yp)
     X.Y2(3)
+    T.own_y(x2)
     L.ring(1, 3)
+    X.S(y2)
+    p(0, y2)
+    loads[2].wait()
+    finish_rows(0)
+    L.rest(0, 2)
+    L.rest(0, 3)
+    L.rest(1, 2)
+    p(1, x)
+    p(1, xp)
+    L.rest(1, 3)
+    T.share_x(yp)
     T.share_x(ym)
     T.share_x(y2)
-    for b in range(8): L.rest(b // 4, b % 4)
-
-    def gather_dot(lhs, rhs, yy):
-        @pl.loop(0, 2)
-        def _(i):
-            k = 2 * yy + i
-            acc[...] += jnp.dot(lhs[k].reshape(256, 1024),
-                                rhs[pl.ds(4 * k, 4)].reshape(1024, 512),
-                                preferred_element_type=F32)
-
-    acc[...] = jnp.zeros_like(acc)
-    X.S(y)
-    gather_dot(Lp, Xp, y)
-    X.S(ym)
-    gather_dot(Lp, Xp, ym)
-    X.S(yp)
-    gather_dot(Lp, Xp, yp)
-    X.S(y2)
-    gather_dot(Lp, Xp, y2)
-
-    loads[2].wait()
-    nw = Wv[...] - 0.01 * acc[...]
-    Np[2 * zl + c] = nw.astype(BF)
-    N.own()
-    Wv[...] = nw
-    store_nw = pltpu.make_async_copy(Wv, nw_hbm, ld.at[6])
-    store_nw.start()
-
-    def out_dot(j, first):
-        zb = zorder[j]
-        lhs = Tq[:, :, :, pl.ds(pl.multiple_of(512 * zb, 512), 512)].reshape(512, 512)
-        v = jnp.dot(lhs, Np[pl.ds(2 * zb, 2)].reshape(512, 512), preferred_element_type=F32)
-        if first:
-            oacc[...] = v
-        else:
-            oacc[...] += v
-
-    for cp in tloads:
-        cp.wait()
+    p(1, xm)
+    p(1, x2)
+    finish_rows(1)
+    for cp in tloads: cp.wait()
     N.Z12()
     T.rest()
     N.S(0)
@@ -425,7 +453,7 @@
     part = oacc[...].reshape(4, 4, 32, 512)
     for q in range(4):
         Ob[q] = part[:, q].reshape(128, 512).astype(BF)
-    for k, (q, d) in enumerate(((yp, D_yp), (ym, D_ym), (y2, D_y2))):
+    for k, (q, d) in enumerate(((y2, D_y2), (yp, D_yp), (ym, D_ym))):
         cp = pltpu.make_async_remote_copy(
             src_ref=Ob.at[q], dst_ref=Ib.at[y], send_sem=so.at[k], recv_sem=ro.at[y],
             device_id=d, device_id_type=MESH)
@@ -438,8 +466,8 @@
     for q in (yp, ym, y2):
       wait_recv(Ib.at[q], ro.at[q])
     Ov[...] = (acc[pl.ds(0, 128)] + Ib[yp].astype(F32) + Ib[ym].astype(F32)
-               + Ib[y2].astype(F32)).astype(BF)
-    store_out = pltpu.make_async_copy(Ov, out_hbm, ld.at[7])
+              + Ib[y2].astype(F32)).astype(BF)
+    store_out = pltpu.make_async_copy(Ov, out_hbm, ld.at[3])
     store_out.start()
     for src, sem, cond in pending:
         if isinstance(src, tuple):
@@ -452,14 +480,28 @@
             cp.wait_send()
         else:
             pl.when(cond)(cp.wait_send)
-    store_nw.wait()
+    for cp in stores:
+        cp.wait()
     store_out.wait()
+
+
+def place(a_hbm, b_hbm, c_hbm, d_hbm, a, b, sem):
+    parts = [(a_hbm, a, c_hbm, pl.ds(64 * q, 64)) for q in range(4)] + [(b_hbm, b, d_hbm, pl.ds(0, 128))]
+    takes = [pltpu.make_async_copy(s.at[r], v.at[r], sem.at[k]) for k, (s, v, o, r) in enumerate(parts)]
+    puts = [pltpu.make_async_copy(v.at[r], o.at[r], sem.at[5 + k]) for k, (s, v, o, r) in enumerate(parts)]
+    for cp in takes:
+        cp.start()
+    for t, p in zip(takes, puts):
+        t.wait()
+        p.start()
+    for cp in puts:
+        cp.wait()
 
 
 def shards(weight, grad, left, right, tokens):
     any_ = pl.BlockSpec(memory_space=pl.ANY)
     dma = pltpu.SemaphoreType.DMA
-    return pl.pallas_call(
+    new_weight, output = pl.pallas_call(
         kernel,
         out_shape=(jax.ShapeDtypeStruct((256, 512), F32), jax.ShapeDtypeStruct((128, 512), BF)),
         in_specs=[any_] * 5,
@@ -483,6 +525,13 @@
         compiler_params=pltpu.CompilerParams(
             collective_id=0, has_side_effects=True, vmem_limit_bytes=56 * 2**20),
     )(weight, grad, left, right, tokens)
+    return pl.pallas_call(
+        place,
+        out_shape=(jax.ShapeDtypeStruct((256, 512), F32), jax.ShapeDtypeStruct((128, 512), BF)),
+        in_specs=[any_] * 2,
+        out_specs=(any_, any_),
+        scratch_shapes=[pltpu.VMEM((256, 512), F32), pltpu.VMEM((128, 512), BF), dma((10,))],
+    )(new_weight, output)
 
 
 def solution(mesh):

time: 130 us -> 120 us (0.923)
  Pallas kernels: 126 us -> 119 us
  local copies, waits for them, and re-layouts: 3.44 us -> 0 us
    pallas_call x1, Pallas kernels: 126 us -> 117 us  [shards(): pl.pallas_call(kernel, out_shape=(jax.ShapeDtypeStruct((256, 512), F32),...]
    unnamed x2 -> x0, local copies, waits for them, and re-layouts: 3.44 us -> none
    pallas_call x0 -> x1, Pallas kernels: none -> 1.91 us  [shards(): pl.pallas_call(place, out_shape=(jax.ShapeDtypeStruct((256, 512), F32), j...]
where the time goes in v3:
time: 120 us
  Pallas kernels  119 us (99%)
    pallas_call x1, Pallas kernels, shards(): pl.pallas_call(kernel, out_shape=(jax.ShapeDtypeStruct((256, 512), F32),...  117 us

profile of v3, /device:TPU:1, one launch (start us, length us, event | category | flops | bytes accessed | tf_op | source)
XLA Modules:
  0.0 119.6 jit_solution(13061891898428016119)
XLA Ops:
  0.6 117.1 %shard_map.68 = (f32[256,512]{1,0:T(8,128)}, bf16[128,512]{1,0:T(8,128)(2,1)}) custom-call(f32[256,512]{1,0:T(8,128)} %w_hbm.1, bf16[256,512]{1,0:T(8,128)(2,1)} %g_hbm.1, bf16[256,1024]{1,0:T(8,128)(2,1)} %l_hbm.1, bf16[128,512]{1,0:T(8,128)(2,1)} %r_hbm.1, bf16[128,8192]{1,0:T(8,128)(2,1)} %t_hbm.1), custom_call_target="tpu_custom_call" | custom-call | tf_op jit(solution)/shard_map/pallas_call | solution.py:504
  117.7 1.9 %shard_map.69 = (f32[256,512]{1,0:T(8,128)}, bf16[128,512]{1,0:T(8,128)(2,1)}) custom-call(f32[256,512]{1,0:T(8,128)} %get-tuple-element.4.a_hbm, bf16[128,512]{1,0:T(8,128)(2,1)} %get-tuple-element.5.b_hbm), custom_call_target="tpu_custom_call" | custom-call | tf_op jit(solution)/shard_map/pallas_call | solution.py:528

commit v4 on v3

--- a/solution.py
+++ b/solution.py
@@ -82,6 +82,8 @@
         zinfo.append((zb, jnp.where(right, zl < 3, zl > 0),
                       dev(z_=jnp.clip(zl + jnp.where(right, 1, -1), 0, 3))))
 
+    mid = (zl + 1) // 2 == 1
+
     class Rho:
         def __init__(self, buf, rows, ss, rs):
             self.buf, self.half, self.ss, self.rs = buf, rows // 2, ss, rs
@@ -163,8 +165,6 @@
             self.sib(("y2", j), i)
 
         def zy(self):
-            mid = (zl + 1) // 2 == 1
-
             @pl.when(mid)
             def _():
                 self.Z12()
@@ -175,6 +175,28 @@
             def _():
                 self.Z(1)
                 self.Y(0)
+                self.Z(2)
+                self.Y(1)
+                self.Z(3)
+
+        def zya(self):
+            @pl.when(mid)
+            def _():
+                self.Z12()
+
+            @pl.when(jnp.logical_not(mid))
+            def _():
+                self.Z(1)
+                self.Y(0)
+
+        def zyb(self):
+            @pl.when(mid)
+            def _():
+                self.Y(0)
+                self.Z(3)
+
+            @pl.when(jnp.logical_not(mid))
+            def _():
                 self.Z(2)
                 self.Y(1)
                 self.Z(3)
@@ -256,44 +278,70 @@
                     wait_recv(Tq.at[r, q], rt.at[r, q])
 
     class Nar:
-        n = 0
-
-        def put(self, i, h, d, cond=None):
-            send(Np.at[i, pl.ds(128 * h, 128)], sn, self.n, rn.at[h, i], d, cond)
-            self.n += 1
-
-        def sib(self, i):
-            send(Np.at[i], sn, self.n, rn.at[0, i], D_sib)
-            self.n += 1
+        keys = {}
+
+        def send(self, key, src, rs, d, cond=None):
+            fresh = key not in self.keys
+            k = self.keys.setdefault(key, len(self.keys))
+            cp = pltpu.make_async_remote_copy(
+                src_ref=src, dst_ref=src, send_sem=sn.at[k], recv_sem=rs,
+                device_id=d, device_id_type=MESH)
+            if cond is None:
+                cp.start()
+            else:
+                pl.when(cond)(cp.start)
+            if fresh:
+                pending.append(((Np, None if key[1] == "s" else 128), (sn, k), cond))
+
+        def put(self, key, i, h, d, cond):
+            self.send((key, h), Np.at[i, pl.ds(128 * h, 128)], rn.at[h, i], d, cond)
+
+        def sib(self, j):
+            i = 2 * zorder[j] + c
+            self.send((j, "s"), Np.at[i], rn.at[0, i], D_sib)
 
         def own(self, h):
             i = 2 * zl + c
-            self.put(i, h, D_zr, zl < 3)
-            self.put(i, h, D_zl, zl > 0)
+            self.put("r", i, h, D_zr, zl < 3)
+            self.put("l", i, h, D_zl, zl > 0)
             if h == 1:
-                self.sib(i)
+                self.sib(0)
 
         def zpart(self, j, h):
             zb, ok, d = zinfo[j]
             i = 2 * zb + c
             wait_recv(Np.at[i, pl.ds(128 * h, 128)], rn.at[h, i])
-            self.put(i, h, d, ok)
-
-        def Z12(self):
-            for h in range(2):
-                self.zpart(1, h)
-                self.zpart(2, h)
-            self.sib(2 * zorder[1] + c)
-            self.sib(2 * zorder[2] + c)
-
-        def Z3(self):
-            self.zpart(3, 0)
-            self.zpart(3, 1)
-            self.sib(2 * zorder[3] + c)
+            self.put(("z", j), i, h, d, ok)
+            if h == 1:
+                self.sib(j)
 
         def S(self, j):
             i = 2 * zorder[j] + 1 - c
             wait_recv(Np.at[i], rn.at[0, i])
+
+        def dots(self, js):
+            for j in js:
+                self.S(j)
+                out_dot(j, j == 0)
+
+        def all(self):
+            for j in (1, 2, 3):
+                self.zpart(j, 0)
+            self.zpart(1, 1)
+            self.zpart(2, 1)
+
+            @pl.when(mid)
+            def _():
+                self.zpart(3, 1)
+                T.rest()
+                self.dots((0, 1, 2, 3))
+
+            @pl.when(jnp.logical_not(mid))
+            def _():
+                T.rest()
+                self.dots((0, 1, 2))
+                self.zpart(3, 1)
+                self.dots((3,))
 
     R = Rho(Rp, 128, sr, rr)
     X = Rho(Xp, 256, sx, rx)
@@ -378,10 +426,10 @@
     R.S(y2)
     G.rest(0, 0)
     G.rest(1, 0)
-    G.ring(1, 1)
     x_part(0, zh)
     x_part(0, 1 - zh)
     x_done(0)
+    G.ring(1, 1)
     G.rest(0, 1)
     x_part(1, zh)
     G.rest(1, 1)
@@ -392,18 +440,19 @@
     L.ring(0, 0)
     L.ring(0, 1)
     L.partner(0)
-    X.zy()
+    X.zya()
+    L.partner(1)
+    X.zyb()
     L.own_zh(2)
-    L.partner(1)
     L.ring(0, 2)
     L.ring(0, 3)
     X.y1()
+    X.Y2(0)
+    L.own_zh(3)
+    X.Y(2)
     L.ring(1, 0)
     L.ring(1, 1)
-    X.Y2(0)
-    L.own_zh(3)
     L.partner(2)
-    X.Y(2)
     X.Y2(1)
     X.Y(3)
     L.ring(1, 2)
@@ -439,17 +488,7 @@
     p(1, x2)
     finish_rows(1)
     for cp in tloads: cp.wait()
-    N.Z12()
-    T.rest()
-    N.S(0)
-    out_dot(0, True)
-    N.S(1)
-    out_dot(1, False)
-    N.S(2)
-    out_dot(2, False)
-    N.Z3()
-    N.S(3)
-    out_dot(3, False)
+    N.all()
     part = oacc[...].reshape(4, 4, 32, 512)
     for q in range(4):
         Ob[q] = part[:, q].reshape(128, 512).astype(BF)

time: 120 us -> 119 us (level)
  no operation moved by 1% of the time
where the time goes in v4:
time: 119 us
  Pallas kernels  118 us (99%)
    pallas_call x1, Pallas kernels, shards(): pl.pallas_call(kernel, out_shape=(jax.ShapeDtypeStruct((256, 512), F32),...  116 us

profile of v4, /device:TPU:1, one launch (start us, length us, event | category | flops | bytes accessed | tf_op | source)
XLA Modules:
  0.0 118.6 jit_solution(8089673364553279454)
XLA Ops:
  0.6 116.1 %shard_map.68 = (f32[256,512]{1,0:T(8,128)}, bf16[128,512]{1,0:T(8,128)(2,1)}) custom-call(f32[256,512]{1,0:T(8,128)} %w_hbm.1, bf16[256,512]{1,0:T(8,128)(2,1)} %g_hbm.1, bf16[256,1024]{1,0:T(8,128)(2,1)} %l_hbm.1, bf16[128,512]{1,0:T(8,128)(2,1)} %r_hbm.1, bf16[128,8192]{1,0:T(8,128)(2,1)} %t_hbm.1), custom_call_target="tpu_custom_call" | custom-call | tf_op jit(solution)/shard_map/pallas_call | solution.py:543
  116.7 1.9 %shard_map.69 = (f32[256,512]{1,0:T(8,128)}, bf16[128,512]{1,0:T(8,128)(2,1)}) custom-call(f32[256,512]{1,0:T(8,128)} %get-tuple-element.4.a_hbm, bf16[128,512]{1,0:T(8,128)(2,1)} %get-tuple-element.5.b_hbm), custom_call_target="tpu_custom_call" | custom-call | tf_op jit(solution)/shard_map/pallas_call | solution.py:567

commit v5 on v4

--- a/solution.py
+++ b/solution.py
@@ -352,11 +352,10 @@
 
 
     def x_part(h, hb):
-        @pl.loop(0, 4)
-        def _(q):
-            k = 2 * q + hb
-            acc[pl.ds(128 * h, 128)] += jnp.dot(
-                Gp[k, h], Rp[pl.ds(4 * k, 4)].reshape(512, 512), preferred_element_type=F32)
+        lhs = jnp.concatenate([Gp[2 * q + hb, h] for q in range(4)], axis=1)
+        rhs = jnp.concatenate(
+            [Rp[pl.ds(4 * (2 * q + hb), 4)].reshape(512, 512) for q in range(4)], axis=0)
+        acc[pl.ds(128 * h, 128)] += jnp.dot(lhs, rhs, preferred_element_type=F32)
 
     def x_done(h):
         Xp[me, pl.ds(128 * h, 128)] = acc[pl.ds(128 * h, 128)].astype(BF)
@@ -364,12 +363,11 @@
         X.own(h)
 
     def p(h, yy):
-        @pl.loop(0, 2)
-        def _(i):
-            k = 2 * yy + i
-            acc[pl.ds(128 * h, 128)] += jnp.dot(
-                Lp[k, pl.ds(2 * h, 2)].reshape(128, 1024),
-                Xp[pl.ds(4 * k, 4)].reshape(1024, 512), preferred_element_type=F32)
+        rows = pl.ds(2 * h, 2)
+        lhs = jnp.concatenate(
+            [Lp[2 * yy + i, rows].reshape(128, 1024) for i in range(2)], axis=1)
+        acc[pl.ds(128 * h, 128)] += jnp.dot(
+            lhs, Xp[pl.ds(8 * yy, 8)].reshape(2048, 512), preferred_element_type=F32)
 
     stores = []
 
@@ -481,12 +479,12 @@
     p(1, x)
     p(1, xp)
     L.rest(1, 3)
+    p(1, xm)
+    p(1, x2)
+    finish_rows(1)
     T.share_x(yp)
     T.share_x(ym)
     T.share_x(y2)
-    p(1, xm)
-    p(1, x2)
-    finish_rows(1)
     for cp in tloads: cp.wait()
     N.all()
     part = oacc[...].reshape(4, 4, 32, 512)

time: 119 us -> 118 us (level)
  no operation moved by 1% of the time
where the time goes in v5:
time: 118 us
  Pallas kernels  117 us (99%)
    pallas_call x1, Pallas kernels, shards(): pl.pallas_call(kernel, out_shape=(jax.ShapeDtypeStruct((256, 512), F32),...  115 us

profile of v5, /device:TPU:1, one launch (start us, length us, event | category | flops | bytes accessed | tf_op | source)
XLA Modules:
  0.0 117.9 jit_solution(14617057713134426577)
XLA Ops:
  0.6 115.4 %shard_map.68 = (f32[256,512]{1,0:T(8,128)}, bf16[128,512]{1,0:T(8,128)(2,1)}) custom-call(f32[256,512]{1,0:T(8,128)} %w_hbm.1, bf16[256,512]{1,0:T(8,128)(2,1)} %g_hbm.1, bf16[256,1024]{1,0:T(8,128)(2,1)} %l_hbm.1, bf16[128,512]{1,0:T(8,128)(2,1)} %r_hbm.1, bf16[128,8192]{1,0:T(8,128)(2,1)} %t_hbm.1), custom_call_target="tpu_custom_call" | custom-call | tf_op jit(solution)/shard_map/pallas_call | solution.py:541
  116.0 1.9 %shard_map.69 = (f32[256,512]{1,0:T(8,128)}, bf16[128,512]{1,0:T(8,128)(2,1)}) custom-call(f32[256,512]{1,0:T(8,128)} %get-tuple-element.4.a_hbm, bf16[128,512]{1,0:T(8,128)(2,1)} %get-tuple-element.5.b_hbm), custom_call_target="tpu_custom_call" | custom-call | tf_op jit(solution)/shard_map/pallas_call | solution.py:565
